TPU v7x, 256 devices: a whole 4x4x8 slice. The times are simulated.
256 devices in a mesh: dp: 32 (over z_hi, x, core), tensor: 8 (over z_lo, y).
Axes of the slice: x: 4, y: 4, z: 8 (z_hi: 4, z_lo: 2; z = z_hi * 2 + z_lo), core: 2. Of those that a mesh axis runs over, the one named last changes fastest.
Arguments:
- quant_rows: int32 [32768, 2048], P(('dp', 'tensor')), may hold values from -127 to 127
- residual: bfloat16 [32768, 2048], P(('dp', 'tensor')), may hold values from -48 to 48
- row_scale: float32 [32768], P(('dp', 'tensor')), may hold values from 0.004 to 0.04
- norm_gain: float32 [2048], replicated, may hold values from 0.1 to 1.9
- gate_pre: bfloat16 [32768, 7168], P('dp', 'tensor'), may hold values from -6 to 6
- up_pre: bfloat16 [32768, 7168], P('dp', 'tensor'), may hold values from -6 to 6
- hidden_grad: bfloat16 [32768, 7168], P('dp', 'tensor'), may hold values from -6 to 6
- gate_weight: bfloat16 [2048, 7168], P('dp', 'tensor'), may hold values from -0.125 to 0.125
- up_weight: bfloat16 [2048, 7168], P('dp', 'tensor'), may hold values from -0.125 to 0.125
Outputs:
- resid_grad: bfloat16 [32768, 2048], P(('dp', 'tensor'))
- gate_weight_grad: float32 [2048, 7168], P('dp', 'tensor')
- up_weight_grad: float32 [2048, 7168], P('dp', 'tensor')
All inputs are finite; a program needn't handle non-finite values.
Results may differ from a plain program's by a relative error of at most 0.014.
Values may be sent and summed in bfloat16 or wider, within the bound.
No kernel may reach another device: no remote copies, remote signals or barrier semaphores. Data moves between devices by JAX's collectives and lax.ppermute only.
A program may use at most 64 MiB of HBM per device.

v0:
```python
import math
import jax
import jax.numpy as jnp
from jax import lax
from jax.sharding import PartitionSpec as P


def body(
    quant_rows,
    residual,
    row_scale,
    norm_gain,
    gate_pre,
    up_pre,
    hidden_grad,
    gate_weight,
    up_weight,
):
    summed_in = residual.astype(jnp.float32) + quant_rows.astype(jnp.float32) * row_scale[:, None]
    inverse = lax.rsqrt(jnp.mean(summed_in * summed_in, axis=-1, keepdims=True) + 1e-05)
    unit_rows = summed_in * inverse
    normed = (unit_rows * norm_gain).astype(jnp.bfloat16)
    gathered = lax.all_gather(normed, "tensor", axis=0, tiled=True)
    gate_val = gate_pre.astype(jnp.float32)
    up_val = up_pre.astype(jnp.float32)
    grad_val = hidden_grad.astype(jnp.float32)
    sigmoid_gate = jax.nn.sigmoid(gate_val)
    up_grad = (grad_val * gate_val * sigmoid_gate).astype(jnp.bfloat16)
    gate_grad = (grad_val * up_val * sigmoid_gate * (1.0 + gate_val * (1.0 - sigmoid_gate))).astype(
        jnp.bfloat16
    )
    grad_cat = jnp.concatenate((gate_grad, up_grad), axis=1)
    weight_cat = jnp.concatenate((gate_weight, up_weight), axis=1)
    partial_value = jnp.einsum(
        "rf,nf->rn",
        grad_cat,
        lax.all_gather(weight_cat, "dp", axis=0, tiled=True),
        preferred_element_type=jnp.float32,
    )
    normed_grad = lax.psum_scatter(
        partial_value.astype(jnp.bfloat16), "tensor", scatter_dimension=0, tiled=True
    ).astype(jnp.float32)
    grad_term = norm_gain * normed_grad
    input_grad = inverse * (
        grad_term - unit_rows * jnp.mean(unit_rows * grad_term, axis=-1, keepdims=True)
    )
    resid_grad = input_grad.astype(jnp.bfloat16)
    tokens_all = gate_pre.shape[0] * lax.axis_size("dp")
    factor = 1.0 / math.sqrt(tokens_all)
    weight_part = lax.dot_general(
        gathered, grad_cat, (((0,), (0,)), ((), ())), preferred_element_type=jnp.float32
    )
    own_rows = lax.psum_scatter(
        weight_part.astype(jnp.bfloat16), "dp", scatter_dimension=0, tiled=True
    ).astype(jnp.float32)
    scaled_grad = own_rows * factor
    hidden_width = gate_weight.shape[1]
    return (resid_grad, scaled_grad[:, :hidden_width], scaled_grad[:, hidden_width:])


def solution(mesh):
    placed = (
        P(("dp", "tensor"), None),
        P(("dp", "tensor"), None),
        P(("dp", "tensor")),
        P(),
        P("dp", "tensor"),
        P("dp", "tensor"),
        P("dp", "tensor"),
        P("dp", "tensor"),
        P("dp", "tensor"),
    )
    return jax.shard_map(
        body,
        mesh=mesh,
        in_specs=placed,
        out_specs=(P(("dp", "tensor"), None), P("dp", "tensor"), P("dp", "tensor")),
        check_vma=False,
    )
```

profile of v0, /device:TPU:8, one launch (start us, length us, event | category | flops | bytes accessed | tf_op | source)
XLA Modules:
  0.0 346.1 jit_solution(7484512502405937982)
XLA Ops:
  7.2 0.0 all-gather.3.cloned.1.call-start
  7.2 1.7 pad_maximum_fusion.3
  8.9 0.0 all-gather.3.cloned.1.call-update
  8.9 0.0 reduce-scatter.3.cloned.1.call-start
  8.9 4.7 %fusion.2 = (bf16[1024,896]{1,0:T(8,128)(2,1)S(1)}, bf16[1024,896]{1,0:T(8,128)(2,1)}) fusion(bf16[1024,896]{1,0:T(8,128)(2,1)} %param.15, bf16[1024,896]{1,0:T(8,128)(2,1)} %param.13, bf16[1024,896]{1,0:T(8,128)(2,1)} %param.14), kind=kLoop, calls=%fused_computation.8 | loop fusion | flops 14680064 | bytes 9175040 | tf_op jit(solution)/shard_map/convert_element_type | solution.py:29
  13.6 72.9 %all-gather.3.cloned.1.call-done = bf16[2048,1792]{1,0:T(8,128)(2,1)} async-done(((bf16[64,1792]{1,0:T(8,128)(2,1)}), bf16[2048,1792]{1,0:T(8,128)(2,1)}) %all-gather.3.cloned.1.call-update) | async-done | bytes 7340048 | tf_op jit(solution)/shard_map/all_gather | solution.py:37
  86.5 12.0 %convolution_convert_fusion.1 = bf16[1024,2048]{1,0:T(8,128)(2,1)} fusion(bf16[2048,1792]{1,0:T(8,128)(2,1)} %all-gather.3.cloned.1.call-done, bf16[1024,896]{1,0:T(8,128)(2,1)} %get-tuple-element.4, bf16[1024,896]{1,0:T(8,128)(2,1)S(1)} %get-tuple-element.3), kind=kOutput, calls=%fused_computation.5 | convolution fusion | flops 7525629952 | bytes 15204352 | tf_op jit(solution)/shard_map/rf,nf->rn/dot_general | solution.py:34
  98.5 0.0 copy-start.2
  98.5 0.0 reduce-scatter.3.cloned.1.call-update
  98.5 0.0 all-gather.5.cloned.1.call-start
  98.6 1.1 copy-done
  99.7 0.1 copy-done.1
  99.8 0.3 multiply_reduce_fusion.1
  100.2 51.9 %reduce-scatter.3.cloned.1.call-done = bf16[128,2048]{1,0:T(8,128)(2,1)} async-done(((bf16[1024,2048]{1,0:T(8,128)(2,1)}), bf16[128,2048]{1,0:T(8,128)(2,1)}) %reduce-scatter.3.cloned.1.call-update) | async-done | bytes 524304 | tf_op jit(solution)/shard_map/reduce_scatter | solution.py:40
  152.1 1.5 multiply_reduce_fusion
  153.6 2.5 multiply_convert_fusion
  156.1 0.0 all-gather.5.cloned.1.call-update
  156.2 0.0 reduce-scatter.5.cloned.1.call-start
  156.2 53.9 %all-gather.5.cloned.1.call-done = bf16[1024,2048]{1,0:T(8,128)(2,1)} async-done(((bf16[128,2048]{1,0:T(8,128)(2,1)}), bf16[1024,2048]{1,0:T(8,128)(2,1)}) %all-gather.5.cloned.1.call-update) | async-done | bytes 4194320 | tf_op jit(solution)/shard_map/all_gather | solution.py:23
  210.1 12.1 %convolution_convert_fusion = bf16[2048,1792]{1,0:T(8,128)(2,1)} fusion(bf16[1024,2048]{1,0:T(8,128)(2,1)} %all-gather.5.cloned.1.call-done, bf16[1024,896]{1,0:T(8,128)(2,1)} %get-tuple-element.4, bf16[1024,896]{1,0:T(8,128)(2,1)S(1)} %get-tuple-element.3), kind=kOutput, calls=%fused_computation | convolution fusion | flops 7527202816 | bytes 15204352 | tf_op jit(solution)/shard_map/dot_general | solution.py:50
  222.2 0.0 reduce-scatter.5.cloned.1.call-update
  222.2 115.6 %reduce-scatter.5.cloned.1.call-done = bf16[64,1792]{1,0:T(8,128)(2,1)} async-done(((bf16[2048,1792]{1,0:T(8,128)(2,1)}), bf16[64,1792]{1,0:T(8,128)(2,1)}) %reduce-scatter.5.cloned.1.call-update) | async-done | bytes 229392 | tf_op jit(solution)/shard_map/reduce_scatter | solution.py:53
  337.8 1.0 convert_multiply_fusion.4
  338.8 0.8 fusion.11
  (7 shorter events, 0.0 us)
Async XLA Ops:
  7.2 79.3 %all-gather.3.cloned.1.call-start = ((), (), s32[]{:S(2)}) async-start(), calls=%async_computation.2 | async-start | bytes 7569408 | tf_op jit(solution)/shard_map/all_gather | solution.py:37
  8.9 143.2 %reduce-scatter.3.cloned.1.call-start = ((), (), s32[]{:S(2)}) async-start(), calls=%async_computation.3 | async-start | bytes 4718592 | tf_op jit(solution)/shard_map/reduce_scatter | solution.py:40
  98.5 1.2 copy-start
  98.5 1.4 copy-start.1
  98.5 1.4 copy-start.3
  98.5 53.6 %copy-start.2 = (f32[2048]{0:T(1024)S(1)}, f32[2048]{0:T(1024)}, u32[]{:S(2)}) copy-start(f32[2048]{0:T(1024)} %param.12) | copy-start | bytes 24580
  98.5 111.6 %all-gather.5.cloned.1.call-start = ((), (), s32[]{:S(2)}) async-start(), calls=%async_computation.4 | async-start | bytes 4718592 | tf_op jit(solution)/shard_map/all_gather | solution.py:23
  156.2 181.6 %reduce-scatter.5.cloned.1.call-start = ((), (), s32[]{:S(2)}) async-start(), calls=%async_computation.5 | async-start | bytes 7569408 | tf_op jit(solution)/shard_map/reduce_scatter | solution.py:53
Sparse Core Ops, SparseCore 0:
  11.1 75.3 all-gather.2
  98.6 53.4 reduce-scatter.2
  156.3 53.8 all-gather.4
  222.3 115.4 reduce-scatter.4
where the time goes:
time: 346 us
  waiting for transfers between devices  294 us (85%)
  matrix products  24.1 us (7%)
  between operations  13.8 us (4%)
  other arithmetic  11.7 us (3%)
    reduce_scatter x1, waiting for transfers between devices, body(): lax.psum_scatter(weight_part.astype(jnp.bfloat16), 'dp', scatter_dimensio...  116 us
    all_gather x1, waiting for transfers between devices, body(): lax.all_gather(weight_cat, 'dp', axis=0, tiled=True)  72.9 us
    all_gather x1, waiting for transfers between devices, body(): gathered = lax.all_gather(normed, 'tensor', axis=0, tiled=True)  53.9 us
    reduce_scatter x1, waiting for transfers between devices, body(): lax.psum_scatter(partial_value.astype(jnp.bfloat16), 'tensor', scatter_di...  51.9 us
    dot_general x1, matrix products, body(): lax.dot_general(gathered, grad_cat, (((0,), (0,)), ((), ())), preferred_e...  12.1 us
    dot_general x1, matrix products, body(): jnp.einsum('rf,nf->rn', grad_cat, lax.all_gather(weight_cat, 'dp', axis=0...  12 us
  transfers between devices with their start and end apart: 4, of which 4 were waited for; matrix products, arithmetic and copies ran while one was open for 1% of the time, Pallas kernels for 0%

commit v1 on v0

--- a/solution.py
+++ b/solution.py
@@ -34,7 +34,9 @@
     partial_value = jnp.einsum(
         "rf,nf->rn",
         grad_cat,
-        lax.all_gather(weight_cat, "dp", axis=0, tiled=True),
+        jnp.concatenate(
+            lax.all_to_all(jnp.stack([weight_cat] * lax.axis_size("dp")), "dp", 0, 0), axis=0
+        ),
         preferred_element_type=jnp.float32,
     )
     normed_grad = lax.psum_scatter(

time: 346 us -> 444 us (1.28)
  waiting for transfers between devices: 294 us -> 377 us
  starting transfers between devices: 0.16 us -> 11.7 us
    all_to_all x0 -> x1, waiting for transfers between devices: none -> 159 us  [body(): lax.all_to_all(jnp.stack([weight_cat] * lax.axis_size('dp')), 'dp', 0, 0)]
    all_gather x1 -> x0, waiting for transfers between devices: 72.9 us -> none  [body(): lax.all_gather(weight_cat, 'dp', axis=0, tiled=True)]
    all_to_all x0 -> x1, starting transfers between devices: none -> 11.6 us  [body(): lax.all_to_all(jnp.stack([weight_cat] * lax.axis_size('dp')), 'dp', 0, 0)]
where the time goes in v1:
time: 444 us
  waiting for transfers between devices  377 us (85%)
  matrix products  24.5 us (6%)
  between operations  13.8 us (3%)
  starting transfers between devices  11.7 us (3%)
  other arithmetic  11 us (2%)
  local copies, waits for them, and re-layouts  5.91 us (1%)
    all_to_all x1, waiting for transfers between devices, body(): lax.all_to_all(jnp.stack([weight_cat] * lax.axis_size('dp')), 'dp', 0, 0)  159 us
    reduce_scatter x1, waiting for transfers between devices, body(): lax.psum_scatter(weight_part.astype(jnp.bfloat16), 'dp', scatter_dimensio...  115 us
    all_gather x1, waiting for transfers between devices, body(): gathered = lax.all_gather(normed, 'tensor', axis=0, tiled=True)  54 us
    reduce_scatter x1, waiting for transfers between devices, body(): lax.psum_scatter(partial_value.astype(jnp.bfloat16), 'tensor', scatter_di...  48.4 us
    dot_general x1, matrix products, body(): jnp.einsum('rf,nf->rn', grad_cat, jnp.concatenate(lax.all_to_all(jnp.stac...  12.5 us
    dot_general x1, matrix products, body(): lax.dot_general(gathered, grad_cat, (((0,), (0,)), ((), ())), preferred_e...  12.1 us
    all_to_all x1, starting transfers between devices, body(): lax.all_to_all(jnp.stack([weight_cat] * lax.axis_size('dp')), 'dp', 0, 0)  11.6 us
  transfers between devices with their start and end apart: 4, of which 4 were waited for; matrix products, arithmetic and copies ran while one was open for 1% of the time, Pallas kernels for 0%

profile of v1, /device:TPU:8, one launch (start us, length us, event | category | flops | bytes accessed | tf_op | source)
XLA Modules:
  0.0 444.2 jit_solution(16059647206609181691)
XLA Ops:
  7.2 1.0 pad_maximum_fusion.3
  8.1 3.8 stack.2
  12.0 11.6 %all-to-all-start = ((bf16[32,64,1792]{2,1,0:T(8,128)(2,1)}), bf16[32,64,1792]{2,1,0:T(8,128)(2,1)}, u32[]{:S(2)}, u32[]{:S(2)}) async-start(bf16[32,64,1792]{2,1,0:T(8,128)(2,1)} %stack.2), calls=%async_computation | async-start | bytes 14680064 | tf_op jit(solution)/shard_map/all_to_all | solution.py:38
  23.6 0.0 reduce-scatter.3.cloned.1.call-start
  23.6 4.7 %fusion.2 = (bf16[1024,896]{1,0:T(8,128)(2,1)}, bf16[1024,896]{1,0:T(8,128)(2,1)}) fusion(bf16[1024,896]{1,0:T(8,128)(2,1)S(1)} %copy-done.2, bf16[1024,896]{1,0:T(8,128)(2,1)} %param.13, bf16[1024,896]{1,0:T(8,128)(2,1)} %param.14), kind=kLoop, calls=%fused_computation.8 | loop fusion | flops 14680064 | bytes 9175040 | tf_op jit(solution)/shard_map/convert_element_type | solution.py:29
  28.3 159.5 %all-to-all-done = bf16[32,64,1792]{2,1,0:T(8,128)(2,1)} async-done(((bf16[32,64,1792]{2,1,0:T(8,128)(2,1)}), bf16[32,64,1792]{2,1,0:T(8,128)(2,1)}, u32[]{:S(2)}, u32[]{:S(2)}) %all-to-all-start) | async-done | bytes 7340064 | tf_op jit(solution)/shard_map/all_to_all | solution.py:38
  187.7 12.5 %convolution_convert_fusion.1 = bf16[1024,2048]{1,0:T(8,128)(2,1)} fusion(bf16[2048,1792]{1,0:T(8,128)(2,1)} %bitcast, bf16[1024,896]{1,0:T(8,128)(2,1)} %get-tuple-element.4, bf16[1024,896]{1,0:T(8,128)(2,1)} %get-tuple-element.3), kind=kOutput, calls=%fused_computation.5 | convolution fusion | flops 7525629952 | bytes 15204352 | tf_op jit(solution)/shard_map/rf,nf->rn/dot_general | solution.py:34
  200.2 0.0 copy-start.4
  200.2 0.0 reduce-scatter.3.cloned.1.call-update
  200.3 0.0 all-gather.2.cloned.1.call-start
  200.3 1.1 copy-done
  201.4 0.1 copy-done.1
  201.6 0.3 multiply_reduce_fusion.1
  201.9 48.4 %reduce-scatter.3.cloned.1.call-done = bf16[128,2048]{1,0:T(8,128)(2,1)} async-done(((bf16[1024,2048]{1,0:T(8,128)(2,1)}), bf16[128,2048]{1,0:T(8,128)(2,1)}) %reduce-scatter.3.cloned.1.call-update) | async-done | bytes 524304 | tf_op jit(solution)/shard_map/reduce_scatter | solution.py:42
  250.3 1.5 multiply_reduce_fusion
  251.8 2.5 multiply_convert_fusion
  254.3 0.0 all-gather.2.cloned.1.call-update
  254.3 0.0 reduce-scatter.5.cloned.1.call-start
  254.4 54.0 %all-gather.2.cloned.1.call-done = bf16[1024,2048]{1,0:T(8,128)(2,1)} async-done(((bf16[128,2048]{1,0:T(8,128)(2,1)}), bf16[1024,2048]{1,0:T(8,128)(2,1)}) %all-gather.2.cloned.1.call-update) | async-done | bytes 4194320 | tf_op jit(solution)/shard_map/all_gather | solution.py:23
  308.3 12.1 %convolution_convert_fusion = bf16[2048,1792]{1,0:T(8,128)(2,1)} fusion(bf16[1024,2048]{1,0:T(8,128)(2,1)} %all-gather.2.cloned.1.call-done, bf16[1024,896]{1,0:T(8,128)(2,1)} %get-tuple-element.4, bf16[1024,896]{1,0:T(8,128)(2,1)S(1)} %copy-done.3), kind=kOutput, calls=%fused_computation | convolution fusion | flops 7527202816 | bytes 15204352 | tf_op jit(solution)/shard_map/dot_general | solution.py:52
  320.4 0.0 reduce-scatter.5.cloned.1.call-update
  320.4 115.4 %reduce-scatter.5.cloned.1.call-done = bf16[64,1792]{1,0:T(8,128)(2,1)} async-done(((bf16[2048,1792]{1,0:T(8,128)(2,1)}), bf16[64,1792]{1,0:T(8,128)(2,1)}) %reduce-scatter.5.cloned.1.call-update) | async-done | bytes 229392 | tf_op jit(solution)/shard_map/reduce_scatter | solution.py:55
  435.9 1.0 convert_multiply_fusion.4
  436.8 0.8 fusion.11
  (11 shorter events, 0.0 us)
Async XLA Ops:
  12.0 11.6 %copy-start.2 = (bf16[1024,896]{1,0:T(8,128)(2,1)S(1)}, bf16[1024,896]{1,0:T(8,128)(2,1)}, u32[]{:S(2)}) copy-start(bf16[1024,896]{1,0:T(8,128)(2,1)} %param.15) | copy-start | bytes 5505028
  12.0 175.7 %all-to-all-start = ((bf16[32,64,1792]{2,1,0:T(8,128)(2,1)}), bf16[32,64,1792]{2,1,0:T(8,128)(2,1)}, u32[]{:S(2)}, u32[]{:S(2)}) async-start(bf16[32,64,1792]{2,1,0:T(8,128)(2,1)} %stack.2), calls=%async_computation | async-start | bytes 14680064 | tf_op jit(solution)/shard_map/all_to_all | solution.py:38
  23.6 226.7 %reduce-scatter.3.cloned.1.call-start = ((), (), s32[]{:S(2)}) async-start(), calls=%async_computation.3 | async-start | bytes 4718592 | tf_op jit(solution)/shard_map/reduce_scatter | solution.py:42
  200.2 1.2 copy-start
  200.2 1.4 copy-start.1
  200.2 1.4 copy-start.5
  200.2 50.1 %copy-start.4 = (f32[2048]{0:T(1024)S(1)}, f32[2048]{0:T(1024)}, u32[]{:S(2)}) copy-start(f32[2048]{0:T(1024)} %param.12) | copy-start | bytes 24580
  200.3 108.1 %copy-start.3 = (bf16[1024,896]{1,0:T(8,128)(2,1)S(1)}, bf16[1024,896]{1,0:T(8,128)(2,1)}, u32[]{:S(2)}) copy-start(bf16[1024,896]{1,0:T(8,128)(2,1)} %get-tuple-element.3) | copy-start | bytes 5505028
  200.3 108.1 %all-gather.2.cloned.1.call-start = ((), (), s32[]{:S(2)}) async-start(), calls=%async_computation.4 | async-start | bytes 4718592 | tf_op jit(solution)/shard_map/all_gather | solution.py:23
  254.3 181.5 %reduce-scatter.5.cloned.1.call-start = ((), (), s32[]{:S(2)}) async-start(), calls=%async_computation.5 | async-start | bytes 7569408 | tf_op jit(solution)/shard_map/reduce_scatter | solution.py:55
Sparse Core Ops, SparseCore 0:
  200.4 49.8 reduce-scatter.2
  254.5 53.8 all-gather.1
  320.5 115.2 reduce-scatter.4
